TPU v7x, 512 devices: a whole 4x4x16 slice. The times are simulated.
512 devices in a mesh: row: 16 (over y, z_hi), col: 32 (over z_lo, x, core).
Axes of the slice: x: 4, y: 4, z: 16 (z_hi: 4, z_lo: 4; z = z_hi * 4 + z_lo), core: 2. Of those that a mesh axis runs over, the one named last changes fastest.
Arguments:
- activations: bfloat16 [512, 28672], P('col', 'row'), may hold values from -6 to 6
- act_basis: bfloat16 [28672, 28672], P('row', 'col'), may hold values from -0.03125 to 0.03125
- out_grads: bfloat16 [512, 8192], P('row', 'col'), may hold values from -0.375 to 0.375
- grad_basis: bfloat16 [8192, 8192], P('col', 'row'), may hold values from -0.0625 to 0.0625
Outputs:
- eigen_lambda: bfloat16 [8192, 28672], P('row', 'col')
All inputs are finite; a program needn't handle non-finite values.
Results may differ from a plain program's by a relative error of at most 0.0058.
Values may be sent and summed in bfloat16 or wider, within the bound.
A program may use at most 64 MiB of HBM per device.

v0:
```python
import jax
import jax.numpy as jnp
from jax import lax
from jax.sharding import PartitionSpec as P

SEQS = 2


def local(activations, act_basis, out_grads, grad_basis):
    act_part = jnp.dot(
        lax.all_gather(activations, "col", axis=0, tiled=True),
        act_basis,
        preferred_element_type=jnp.float32,
    )
    rotated_act = lax.psum(act_part, "row").astype(jnp.bfloat16)
    grad_part = jnp.dot(
        lax.all_gather(out_grads, "row", axis=0, tiled=True),
        grad_basis,
        preferred_element_type=jnp.float32,
    )
    rotated_grad = lax.psum(grad_part, "col").astype(jnp.bfloat16)
    tokens_all = rotated_act.shape[0]
    seq_tokens = tokens_all // SEQS
    act_seq = rotated_act.reshape(SEQS, seq_tokens, rotated_act.shape[1])
    grad_seq = rotated_grad.reshape(SEQS, seq_tokens, rotated_grad.shape[1])
    seq_grad = jnp.einsum("slo,sli->soi", grad_seq, act_seq, preferred_element_type=jnp.float32)
    squared = jnp.sum(seq_grad * seq_grad, axis=0) / SEQS
    return squared.astype(jnp.bfloat16)


def solution(mesh):
    return jax.shard_map(
        local,
        mesh=mesh,
        in_specs=(P("col", "row"), P("row", "col"), P("row", "col"), P("col", "row")),
        out_specs=P("row", "col"),
        check_vma=False,
    )
```

profile of v0, /device:TPU:24, one launch (start us, length us, event | category | flops | bytes accessed | tf_op | source)
XLA Modules:
  0.0 407.6 jit_solution(570457305042580934)
XLA Ops:
  6.5 0.0 copy-start
  6.5 0.0 all-gather.2.cloned.1.call-start
  6.5 0.7 all-gather.2.cloned.1.call-update
  7.3 54.8 %all_gather.6 = bf16[512,256]{1,0:T(8,128)(2,1)S(1)} all-gather(bf16[32,256]{1,0:T(8,128)(2,1)} %param.6), channel_id=1, replica_groups=mesh['row'=16,'col'=32] {'row'}, dimensions={0}, use_global_device_ids=true | all-gather | bytes 278528 | tf_op jit(solution)/shard_map/all_gather | solution.py:17
  62.1 2.2 fusion
  64.3 146.9 %all-reduce.3 = bf16[512,512]{1,0:T(8,128)(2,1)} all-reduce(f32[512,512]{1,0:T(8,128)} %fusion), channel_id=1, replica_groups=mesh['row'=16,'col'=32] {'col'}, use_global_device_ids=true, to_apply=%region_0.0 | all-reduce | flops 262144 | bytes 1572864 | tf_op jit(solution)/shard_map/psum | solution.py:21
  211.3 0.0 all-gather.2.cloned.1.call-done
  211.3 0.0 copy-done
  211.3 4.8 %fusion.1 = f32[512,896]{1,0:T(8,128)} fusion(bf16[512,1792]{1,0:T(8,128)(2,1)} %all-gather.2.cloned.1.call-done, bf16[1792,896]{1,0:T(8,128)(2,1)S(1)} %copy-done), kind=kOutput, calls=%fused_computation.3 | convolution fusion | flops 1644167168 | bytes 6881280 | tf_op jit(solution)/shard_map/dot_general | solution.py:10
  216.0 181.4 %all-reduce.2 = bf16[512,896]{1,0:T(8,128)(2,1)} all-reduce(f32[512,896]{1,0:T(8,128)} %fusion.1), channel_id=1, replica_groups=mesh['row'=16,'col'=32] {'row'}, use_global_device_ids=true, to_apply=%region_1.0 | all-reduce | flops 458752 | bytes 2752512 | tf_op jit(solution)/shard_map/psum | solution.py:15
  397.5 2.3 multiply_reduce_fusion
  399.8 1.0 multiply_convert_fusion
Async XLA Ops:
  6.5 204.7 %copy-start = (bf16[1792,896]{1,0:T(8,128)(2,1)S(1)}, bf16[1792,896]{1,0:T(8,128)(2,1)}, u32[]{:S(2)}) copy-start(bf16[1792,896]{1,0:T(8,128)(2,1)} %param.5) | copy-start | bytes 9633796
  6.5 204.7 %all-gather.2.cloned.1.call-start = ((), (), s32[]{:S(2)}) async-start(), calls=%async_computation | async-start | bytes 1892352 | tf_op jit(solution)/shard_map/all_gather | solution.py:11
Sparse Core Ops, SparseCore 0:
  9.5 69.1 all-gather.1
where the time goes:
time: 408 us
  blocking collectives  383 us (94%)
  between operations  13.4 us (3%)
  matrix products  9.31 us (2%)
    psum x1, blocking collectives, local(): rotated_act = lax.psum(act_part, 'row').astype(jnp.bfloat16)  181 us
    psum x1, blocking collectives, local(): rotated_grad = lax.psum(grad_part, 'col').astype(jnp.bfloat16)  147 us
    all_gather x1, blocking collectives, local(): lax.all_gather(out_grads, 'row', axis=0, tiled=True)  54.8 us
  transfers between devices with their start and end apart: 1, of which 0 were waited for; matrix products, arithmetic and copies ran while one was open for 1% of the time, Pallas kernels for 0%

commit v1 on v0

--- a/solution.py
+++ b/solution.py
@@ -18,7 +18,7 @@
         grad_basis,
         preferred_element_type=jnp.float32,
     )
-    rotated_grad = lax.psum(grad_part, "col").astype(jnp.bfloat16)
+    rotated_grad = jnp.sum(lax.all_gather(grad_part, "col"), axis=0).astype(jnp.bfloat16)
     tokens_all = rotated_act.shape[0]
     seq_tokens = tokens_all // SEQS
     act_seq = rotated_act.reshape(SEQS, seq_tokens, rotated_act.shape[1])

time: 408 us -> 442 us (1.083); the launches traced: 408 us -> 437 us
  waiting for transfers between devices: 0.71 us -> 137 us
  blocking collectives: 383 us -> 264 us
  other arithmetic: 1.05 us -> 14.2 us
    psum x1 -> x0, blocking collectives: 147 us -> none  [local(): rotated_grad = lax.psum(grad_part, 'col').astype(jnp.bfloat16)]
    all_gather x0 -> x1, waiting for transfers between devices: none -> 123 us  [local(): lax.all_gather(grad_part, 'col')]
    psum x1, blocking collectives: 181 us -> 208 us  [local(): rotated_act = lax.psum(act_part, 'row').astype(jnp.bfloat16)]
    all_gather x1, waiting for transfers between devices: 0.01 us -> 13.3 us  [local(): lax.all_gather(activations, 'col', axis=0, tiled=True)]
    reduce_sum x0 -> x1, other arithmetic: none -> 13.1 us  [local(): jnp.sum(lax.all_gather(grad_part, 'col'), axis=0).astype(jnp.bfloat16)]
  transfers between devices with their start and end apart: 1 -> 2, of which waited for: 0 -> 2; matrix products, arithmetic and copies ran while one was open for 1% -> 2% of each run, Pallas kernels for 0% -> 0%
where the time goes in v1:
time: 442 us; the launch traced here: 437 us
  blocking collectives  264 us (60%)
  waiting for transfers between devices  137 us (31%)
  other arithmetic  14.2 us (3%)
  between operations  13.4 us (3%)
  matrix products  9.3 us (2%)
    psum x1, blocking collectives, local(): rotated_act = lax.psum(act_part, 'row').astype(jnp.bfloat16)  208 us
    all_gather x1, waiting for transfers between devices, local(): lax.all_gather(grad_part, 'col')  123 us
    all_gather x1, blocking collectives, local(): lax.all_gather(out_grads, 'row', axis=0, tiled=True)  55.7 us
    all_gather x1, waiting for transfers between devices, local(): lax.all_gather(activations, 'col', axis=0, tiled=True)  13.3 us
    reduce_sum x1, other arithmetic, local(): jnp.sum(lax.all_gather(grad_part, 'col'), axis=0).astype(jnp.bfloat16)  13.1 us
  transfers between devices with their start and end apart: 2, of which 2 were waited for; matrix products, arithmetic and copies ran while one was open for 2% of the time, Pallas kernels for 0%

profile of v1, /device:TPU:24, one launch (start us, length us, event | category | flops | bytes accessed | tf_op | source)
XLA Modules:
  0.0 437.2 jit_solution(2332767530243995575)
XLA Ops:
  6.5 0.0 copy-start
  6.5 0.0 all-gather.4.cloned.1.call-start
  6.5 0.7 all-gather.4.cloned.1.call-update
  7.3 0.0 all-gather.6.cloned.1.call-start
  7.3 55.7 %all_gather.12 = bf16[512,256]{1,0:T(8,128)(2,1)S(1)} all-gather(bf16[32,256]{1,0:T(8,128)(2,1)} %param.6), channel_id=1, replica_groups=mesh['row'=16,'col'=32] {'row'}, dimensions={0}, use_global_device_ids=true | all-gather | bytes 278528 | tf_op jit(solution)/shard_map/all_gather | solution.py:17
  63.0 2.2 fusion
  65.3 0.0 all-gather.6.cloned.1.call-update
  65.3 13.3 %all-gather.4.cloned.1.call-done = bf16[512,1792]{1,0:T(8,128)(2,1)} async-done(((bf16[16,1792]{1,0:T(8,128)(2,1)}), bf16[512,1792]{1,0:T(8,128)(2,1)}) %all-gather.4.cloned.1.call-update) | async-done | bytes 1835024 | tf_op jit(solution)/shard_map/all_gather | solution.py:11
  78.6 0.0 copy-done
  78.6 4.8 %fusion.1 = f32[512,896]{1,0:T(8,128)} fusion(bf16[512,1792]{1,0:T(8,128)(2,1)} %all-gather.4.cloned.1.call-done, bf16[1792,896]{1,0:T(8,128)(2,1)S(1)} %copy-done), kind=kOutput, calls=%fused_computation.3 | convolution fusion | flops 1644167168 | bytes 6881280 | tf_op jit(solution)/shard_map/dot_general | solution.py:10
  83.3 207.9 %all-reduce.1 = bf16[512,896]{1,0:T(8,128)(2,1)} all-reduce(f32[512,896]{1,0:T(8,128)} %fusion.1), channel_id=1, replica_groups=mesh['row'=16,'col'=32] {'row'}, use_global_device_ids=true, to_apply=%region_1.0 | all-reduce | flops 458752 | bytes 2752512 | tf_op jit(solution)/shard_map/psum | solution.py:15
  291.2 122.7 %all-gather.6.cloned.1.call-done = f32[16384,512]{1,0:T(8,128)} async-done(((f32[512,512]{1,0:T(8,128)}), f32[16384,512]{1,0:T(8,128)}) %all-gather.6.cloned.1.call-update) | async-done | bytes 33554448 | tf_op jit(solution)/shard_map/all_gather | solution.py:21
  413.9 13.1 %reduce_sum.18 = bf16[512,512]{1,0:T(8,128)(2,1)} reduce(f32[32,512,512]{2,1,0:T(8,128)} %bitcast.9, f32[]{:T(128)} %constant.1.clone.1), dimensions={0}, to_apply=%region_0.0 | reduce | flops 8126464 | bytes 34078724 | tf_op jit(solution)/shard_map/reduce_sum | solution.py:21
  427.0 2.3 multiply_reduce_fusion
  429.3 1.0 multiply_convert_fusion
Async XLA Ops:
  6.5 72.0 %copy-start = (bf16[1792,896]{1,0:T(8,128)(2,1)S(1)}, bf16[1792,896]{1,0:T(8,128)(2,1)}, u32[]{:S(2)}) copy-start(bf16[1792,896]{1,0:T(8,128)(2,1)} %param.5) | copy-start | bytes 9633796
  6.5 72.0 %all-gather.4.cloned.1.call-start = ((), (), s32[]{:S(2)}) async-start(), calls=%async_computation | async-start | bytes 1892352 | tf_op jit(solution)/shard_map/all_gather | solution.py:11
  7.3 406.7 %all-gather.6.cloned.1.call-start = ((), (), s32[]{:S(2)}) async-start(), calls=%async_computation.1 | async-start | bytes 34603008 | tf_op jit(solution)/shard_map/all_gather | solution.py:21
Sparse Core Ops, SparseCore 0:
  9.5 69.0 all-gather.3
  80.7 333.1 all-gather.5
